TPU v7x, 32 devices: a whole 2x2x4 slice. The times are simulated.
32 devices in a mesh: parts: 2 (over y), patch: 4 (over z), level: 2 (over x), sub: 2 (over core).
Axes of the slice: x: 2, y: 2, z: 4, core: 2. Of those that a mesh axis runs over, the one named last changes fastest.
Arguments:
- adjoint_height: float32 [4, 1024, 1024], P(('parts', 'level'), ('patch', 'sub')), parts along dimension 0, may hold values from -6 to 6
- adjoint_momenta: float32 [2, 4, 1024, 1024], P(None, ('parts', 'level'), ('patch', 'sub')), parts along dimension 1, may hold values from -6 to 6
- depth: float32 [2, 1024, 1024], P('level', ('patch', 'sub')), may hold values from 0.2 to 1
- wet_mask: int32 [2, 1024, 1024], P('level', ('patch', 'sub')), may hold values 0 or 1
- adjacency: int32 [2, 4, 4], P('level'), may hold values from -1 to 3, as said below
- nest_gain: float32 [2, 8192], P(None, ('patch', 'sub')), may hold values from 0.75 to 1
- nest_index: int32 [2, 8192], P(None, ('patch', 'sub')), may hold values from 0 to 1023, as said below
Outputs:
- height_out: float32 [4, 1024, 1024], P(('parts', 'level'), ('patch', 'sub')), parts along dimension 0
- momenta_out: float32 [2, 4, 1024, 1024], P(None, ('parts', 'level'), ('patch', 'sub')), parts along dimension 1
There are 2 independent parts, one for each index of `parts`. A program takes and returns all parts, laid end to end along the dimension named above; an argument that names none is the same for every part. Nothing has to cross between parts.
Inputs may be any that keep to these rules, and one draw needn't show every extreme that they name: `adjacency`: the patches of a level sit on a grid of cells in an order drawn from the seed; each row of a patch lists its grid neighbours, -1 at the grid's edge, and neighbour links are symmetric. `nest_index`: entries index a cell of the same half patch's strip, 1024 cells long.
All inputs are finite; a program needn't handle non-finite values. No bound on the sum of `wet_mask` on one device may be relied on, other than what follows from the above.
Results may differ from a plain program's by a relative error of at most 0.00002.
Values sent between devices are 32-bit elements; how exact they have to be, the bound alone decides.
A program may use at most 64 MiB of HBM per device.

v0:
```python
import jax
import jax.numpy as jnp
from jax import lax
from jax.sharding import PartitionSpec as P

STEPS = 2
courant = 0.45


def passed_along(value, axis, steps):
    count = lax.axis_size(axis)
    initial, last = (max(0, -steps), min(count, count - steps))
    return lax.ppermute(value, axis, [(source, source + steps) for source in range(initial, last)])


def pick_row(table, index):
    return lax.dynamic_index_in_dim(table, index, 0, keepdims=False)


def body(adjoint_height, adjoint_momenta, depth, wet_mask, adjacency, nest_gain, nest_index):
    eta = adjoint_height[0]
    mom_row = adjoint_momenta[0, 0]
    mom_col = adjoint_momenta[1, 0]
    height = depth[0]
    wet = wet_mask[0].astype(jnp.float32)
    level = lax.axis_index("level")
    patch = lax.axis_index("patch")
    half = lax.axis_index("sub")
    levels = lax.axis_size("level")
    subs = lax.axis_size("sub")
    segments = lax.axis_size("patch") * subs
    links = pick_row(adjacency[0], patch)
    north = links[0]
    south = links[1]
    west = links[2]
    east = links[3]
    has_north = (north >= 0).astype(jnp.float32)
    has_south = (south >= 0).astype(jnp.float32)
    has_west = (west >= 0).astype(jnp.float32)
    has_east = (east >= 0).astype(jnp.float32)
    own_gain = pick_row(nest_gain, level)
    own_table = pick_row(nest_index, level)
    for step in range(STEPS):
        strip = eta[0]
        flux = strip
        inflow = jnp.zeros_like(strip)
        for turn in range(levels - 1):
            received = passed_along(flux, "level", -1)
            inflow = own_gain * jnp.take(received, own_table)
            flux = inflow + strip
        eta = eta.at[0].add(inflow)
        first_col = eta[:, 0]
        first_row = eta[0, :]
        east_cols = lax.all_gather(first_col[None], ("patch", "sub"), axis=0, tiled=True)
        east_rows = lax.all_gather(first_row[None], ("patch", "sub"), axis=0, tiled=True)
        east_col = jnp.take(east_cols, jnp.maximum(east, 0) * subs + half, axis=0) * has_east
        east_inside = jnp.take(
            east_rows, jnp.minimum(patch * subs + half + 1, segments - 1), axis=0
        )
        east_across = jnp.take(east_rows, jnp.maximum(south, 0) * subs, axis=0) * has_south
        south_row = jnp.where(half == subs - 1, east_across, east_inside)
        east_col, south_row = (east_col, south_row)
        east_eta = jnp.concatenate([eta[:, 1:], east_col[:, None]], axis=1)
        south_eta = jnp.concatenate([eta[1:], south_row[None]], axis=0)
        mom_row = wet * (mom_row - courant * (east_eta - eta))
        mom_col = wet * (mom_col - courant * (south_eta - eta))
        last_col = mom_row[:, -1]
        last_row = mom_col[-1, :]
        cols = lax.all_gather(last_col[None], ("patch", "sub"), axis=0, tiled=True)
        rows = lax.all_gather(last_row[None], ("patch", "sub"), axis=0, tiled=True)
        west_col = jnp.take(cols, jnp.maximum(west, 0) * subs + half, axis=0) * has_west
        inside = jnp.take(rows, jnp.maximum(patch * subs + half - 1, 0), axis=0)
        across = jnp.take(rows, jnp.maximum(north, 0) * subs + subs - 1, axis=0) * has_north
        north_row = jnp.where(half == 0, across, inside)
        west_col, north_row = (west_col, north_row)
        west_row = jnp.concatenate([west_col[:, None], mom_row[:, :-1]], axis=1)
        north_col = jnp.concatenate([north_row[None], mom_col[:-1]], axis=0)
        eta = wet * (eta - courant * height * (mom_row - west_row + (mom_col - north_col)))
    return (eta[None], jnp.stack([mom_row, mom_col])[:, None])


def solution(mesh):
    in_specs = (
        P(("parts", "level"), ("patch", "sub"), None),
        P(None, ("parts", "level"), ("patch", "sub"), None),
        P("level", ("patch", "sub"), None),
        P("level", ("patch", "sub"), None),
        P("level", None, None),
        P(None, ("patch", "sub")),
        P(None, ("patch", "sub")),
    )
    out_specs = (
        P(("parts", "level"), ("patch", "sub"), None),
        P(None, ("parts", "level"), ("patch", "sub"), None),
    )
    return jax.shard_map(body, mesh=mesh, in_specs=in_specs, out_specs=out_specs, check_vma=False)
```

profile of v0, /device:TPU:0, one launch (start us, length us, event | category | flops | bytes accessed | tf_op | source)
XLA Modules:
  0.0 152.6 jit_solution(2689515999720986161)
XLA Ops:
  0.6 0.0 copy-start
  0.6 1.0 copy.33
  1.7 1.3 collective-permute-start
  3.0 0.7 constant_dynamic-slice_fusion.4
  3.7 0.6 fusion.35
  4.3 0.0 copy-done
  4.3 0.0 copy-start.4
  4.3 0.7 copy-done.4
  10.1 0.0 collective-permute-done
  10.2 4.5 %gather_fusion = f32[1024]{0:T(1024)S(1)} fusion(f32[1024]{0:T(1024)S(1)} %collective-permute-done, s32[1024]{0:T(1024)S(1)} %fusion.22), kind=kCustom, calls=%fused_computation.clone | custom fusion | bytes 12288 | tf_op jit(solution)/shard_map/jit(_take)/gather | solution.py:49
  14.7 15.7 %all-gather.2 = f32[8192]{0:T(1024)S(1)} all-gather(f32[1024]{0:T(1024)S(1)} %get-tuple-element.51), channel_id=4, replica_groups=mesh['parts'=2,'patch'=4,'level'=2,'sub'=2] {'patch','sub'}, dimensions={0}, use_global_device_ids=true | all-gather | bytes 36864 | tf_op jit(solution)/shard_map/all_gather | solution.py:55
  30.4 0.1 scatter-add.6
  30.5 0.2 slice.143
  30.7 0.0 copy-start.1
  30.8 14.8 %all-gather = f32[1024,1]{1,0:T(8,128)S(1)} all-gather(f32[128,1]{1,0:T(8,128)S(1)} %slice.144), channel_id=2, replica_groups=mesh['parts'=2,'patch'=4,'level'=2,'sub'=2] {'patch','sub'}, dimensions={0}, use_global_device_ids=true | all-gather | bytes 4608 | tf_op jit(solution)/shard_map/all_gather | solution.py:54
  45.6 0.2 reduce.4
  45.8 0.1 copy.17
  46.0 0.0 copy-done.1
  46.0 1.6 %fusion.9 = (f32[128,1024]{1,0:T(8,128)S(1)}, f32[128,1024]{1,0:T(8,128)S(1)}) fusion(f32[128,1024]{1,0:T(8,128)S(1)} %scatter-add.6, f32[1,1024]{1,0:T(1,128)S(1)} %bitcast.119, f32[127,1024]{1,0:T(8,128)S(1)} %slice.147, f32[2,1,128,1024]{3,2,1,0:T(8,128)} %param.18, s32[1,128,1024]{2,1,0:T(8,128)S(1)} %copy-done.1, f32[128,1]{1,0:T(8,128)S(1)} %copy.17, ...), kind=kLoop, calls=%fused_computation.15 | loop fusion | flops 1441792 | bytes 4194304 | tf_op jit(solution)/shard_map/mul | solution.py:66
  47.6 14.2 %all-gather.5 = f32[8,1,1024]{2,1,0:T(1,128)S(1)} all-gather(f32[1,1,1024]{2,1,0:T(1,128)S(1)} %slice_bitcast_fusion.1), channel_id=1, replica_groups=mesh['parts'=2,'patch'=4,'level'=2,'sub'=2] {'patch','sub'}, dimensions={0}, use_global_device_ids=true | all-gather | bytes 36864 | tf_op jit(solution)/shard_map/all_gather | solution.py:70
  61.8 0.1 slice.145
  61.9 0.0 copy-start.2
  61.9 15.0 %all-gather.1 = f32[1024,1]{1,0:T(8,128)S(1)} all-gather(f32[128,1]{1,0:T(8,128)S(1)} %slice.145), channel_id=3, replica_groups=mesh['parts'=2,'patch'=4,'level'=2,'sub'=2] {'patch','sub'}, dimensions={0}, use_global_device_ids=true | all-gather | bytes 4608 | tf_op jit(solution)/shard_map/all_gather | solution.py:69
  76.9 0.2 reduce.5
  77.2 0.1 copy.18
  77.3 0.0 copy-done.2
  77.3 0.4 fusion.6
  77.7 1.3 collective-permute-start.1
  79.0 4.2 %collective-permute-done.1 = f32[1024]{0:T(1024)S(1)} collective-permute-done((f32[1024]{0:T(1024)S(1)}, f32[1024]{0:T(1024)S(1)}, u32[]{:S(2)}, u32[]{:S(2)}) %collective-permute-start.1) | collective-permute-done | bytes 4128 | tf_op jit(solution)/shard_map/ppermute | solution.py:13
  83.2 4.5 %gather_fusion.1 = f32[1024]{0:T(1024)S(1)} fusion(f32[1024]{0:T(1024)S(1)} %collective-permute-done.1, s32[1024]{0:T(1024)S(1)} %fusion.22), kind=kCustom, calls=%fused_computation.1.clone | custom fusion | bytes 12288 | tf_op jit(solution)/shard_map/jit(_take)/gather | solution.py:49
  87.8 0.1 scatter-add.9
  87.9 0.8 slice.155
  88.8 1.0 slice.151
  89.8 14.0 %all-gather.6 = f32[8,1,1024]{2,1,0:T(1,128)S(1)} all-gather(f32[1,1,1024]{2,1,0:T(1,128)S(1)} %bitcast.111), channel_id=1, replica_groups=mesh['parts'=2,'patch'=4,'level'=2,'sub'=2] {'patch','sub'}, dimensions={0}, use_global_device_ids=true | all-gather | bytes 36864 | tf_op jit(solution)/shard_map/all_gather | solution.py:55
  103.8 14.9 %all-gather.3 = f32[1024,1]{1,0:T(8,128)S(1)} all-gather(f32[128,1]{1,0:T(8,128)S(1)} %slice.152), channel_id=5, replica_groups=mesh['parts'=2,'patch'=4,'level'=2,'sub'=2] {'patch','sub'}, dimensions={0}, use_global_device_ids=true | all-gather | bytes 4608 | tf_op jit(solution)/shard_map/all_gather | solution.py:54
  118.7 0.2 reduce.6
  118.9 0.1 copy.19
  119.1 1.6 %fusion.20 = (f32[128,1024]{1,0:T(8,128)S(1)}, f32[128,1024]{1,0:T(8,128)S(1)}) fusion(f32[128,1024]{1,0:T(8,128)S(1)} %get-tuple-element.53, f32[128,1024]{1,0:T(8,128)S(1)} %scatter-add.9, f32[1,1024]{1,0:T(1,128)S(1)} %bitcast.117, f32[127,1024]{1,0:T(8,128)} %slice.155, s32[1,128,1024]{2,1,0:T(8,128)S(1)} %copy-done.1, ...), kind=kLoop, calls=%fused_computation.30 | loop fusion | flops 1441792 | bytes 4194304 | tf_op jit(solution)/shard_map/mul | solution.py:66
  120.6 14.3 %all-gather.7 = f32[8,1,1024]{2,1,0:T(1,128)S(1)} all-gather(f32[1,1,1024]{2,1,0:T(1,128)S(1)} %slice_bitcast_fusion), channel_id=1, replica_groups=mesh['parts'=2,'patch'=4,'level'=2,'sub'=2] {'patch','sub'}, dimensions={0}, use_global_device_ids=true | all-gather | bytes 36864 | tf_op jit(solution)/shard_map/all_gather | solution.py:70
  134.9 0.1 slice.153
  135.0 14.9 %all-gather.4 = f32[1024,1]{1,0:T(8,128)S(1)} all-gather(f32[128,1]{1,0:T(8,128)S(1)} %slice.153), channel_id=6, replica_groups=mesh['parts'=2,'patch'=4,'level'=2,'sub'=2] {'patch','sub'}, dimensions={0}, use_global_device_ids=true | all-gather | bytes 4608 | tf_op jit(solution)/shard_map/all_gather | solution.py:69
  149.9 0.2 reduce.7
  150.1 0.1 copy.20
  150.2 0.0 copy-start.3
  150.3 1.1 maximum_bitcast_fusion
  151.3 0.1 copy-done.3
  151.4 1.2 fusion.17
  (29 shorter events, 0.3 us)
Async XLA Ops:
  0.6 3.7 %copy-start = (s32[2,1024]{1,0:T(2,128)S(1)}, s32[2,1024]{1,0:T(2,128)}, u32[]{:S(2)}) copy-start(s32[2,1024]{1,0:T(2,128)} %param.23) | copy-start | bytes 24580
  1.7 8.4 %collective-permute-start = (f32[1024]{0:T(1024)S(1)}, f32[1024]{0:T(1024)S(1)}, u32[]{:S(2)}, u32[]{:S(2)}) collective-permute-start(f32[1024]{0:T(1024)S(1)} %bitcast.122), channel_id=1, source_target_pairs={{2,0},{3,1},{6,4},{7,5},{10,8},{11,9},{14,12},{15,13},{18,16},{19,... | collective-permute-start | bytes 12296 | tf_op jit(solution)/shard_map/ppermute | solution.py:13
  4.3 0.7 copy-start.4
  30.7 15.2 %copy-start.1 = (s32[1,128,1024]{2,1,0:T(8,128)S(1)}, s32[1,128,1024]{2,1,0:T(8,128)}, u32[]{:S(2)}) copy-start(s32[1,128,1024]{2,1,0:T(8,128)} %param.20) | copy-start | bytes 1572868
  61.9 15.4 %copy-start.2 = (f32[1,128,1024]{2,1,0:T(8,128)S(1)}, f32[1,128,1024]{2,1,0:T(8,128)}, u32[]{:S(2)}) copy-start(f32[1,128,1024]{2,1,0:T(8,128)} %param.19) | copy-start | bytes 1572868
  77.7 5.5 %collective-permute-start.1 = (f32[1024]{0:T(1024)S(1)}, f32[1024]{0:T(1024)S(1)}, u32[]{:S(2)}, u32[]{:S(2)}) collective-permute-start(f32[1024]{0:T(1024)S(1)} %bitcast.136), channel_id=1, source_target_pairs={{2,0},{3,1},{6,4},{7,5},{10,8},{11,9},{14,12},{15,13},{18,16},{19,... | collective-permute-start | bytes 12296 | tf_op jit(solution)/shard_map/ppermute | solution.py:13
  150.2 1.1 copy-start.3
where the time goes:
time: 153 us
  blocking collectives  118 us (77%)
  local copies, waits for them, and re-layouts  15.1 us (10%)
  other arithmetic  6.77 us (4%)
  between operations  6.05 us (4%)
  waiting for transfers between devices  4.2 us (3%)
  starting transfers between devices  2.57 us (2%)
    all_gather x2, blocking collectives, body(): cols = lax.all_gather(last_col[None], ('patch', 'sub'), axis=0, tiled=True)  29.9 us
    all_gather x2, blocking collectives, body(): lax.all_gather(first_col[None], ('patch', 'sub'), axis=0, tiled=True)  29.8 us
    all_gather x2, blocking collectives, body(): lax.all_gather(first_row[None], ('patch', 'sub'), axis=0, tiled=True)  29.7 us
    all_gather x2, blocking collectives, body(): rows = lax.all_gather(last_row[None], ('patch', 'sub'), axis=0, tiled=True)  28.5 us
    gather x2, local copies, waits for them, and re-layouts, body(): inflow = own_gain * jnp.take(received, own_table)  9.05 us
    ppermute x2, waiting for transfers between devices, passed_along(): lax.ppermute(value, axis, [(source, source + steps) for source in range(i...  4.2 us
    mul x2, other arithmetic, body(): mom_col = wet * (mom_col - courant * (south_eta - eta))  3.13 us
  transfers between devices with their start and end apart: 2, of which 1 were waited for; matrix products, arithmetic and copies ran while one was open for 1% of the time, Pallas kernels for 0%

commit v1 on v0

--- a/solution.py
+++ b/solution.py
@@ -5,6 +5,25 @@
 
 STEPS = 2
 courant = 0.45
+
+
+def laid_out(blocks, dim):
+    shape = list(blocks.shape[1:])
+    shape[dim] *= blocks.shape[0]
+    return jnp.moveaxis(blocks, 0, dim).reshape(shape)
+
+
+def grow_blocks(x, axis):
+    length, index = (lax.axis_size(axis), lax.axis_index(axis))
+    blocks, stride = (x[None], 1)
+    while stride < length:
+        received = lax.ppermute(blocks, axis, [(i, i ^ stride) for i in range(length)])
+        low = index & stride == 0
+        blocks = jnp.concatenate(
+            [jnp.where(low, blocks, received), jnp.where(low, received, blocks)]
+        )
+        stride *= 2
+    return blocks
 
 
 def passed_along(value, axis, steps):
@@ -67,7 +86,7 @@
         last_col = mom_row[:, -1]
         last_row = mom_col[-1, :]
         cols = lax.all_gather(last_col[None], ("patch", "sub"), axis=0, tiled=True)
-        rows = lax.all_gather(last_row[None], ("patch", "sub"), axis=0, tiled=True)
+        rows = laid_out(grow_blocks(last_row[None], ("patch", "sub")), 0)
         west_col = jnp.take(cols, jnp.maximum(west, 0) * subs + half, axis=0) * has_west
         inside = jnp.take(rows, jnp.maximum(patch * subs + half - 1, 0), axis=0)
         across = jnp.take(rows, jnp.maximum(north, 0) * subs + subs - 1, axis=0) * has_north

time: 153 us -> 138 us (0.902)
  blocking collectives: 118 us -> 88.9 us
  waiting for transfers between devices: 4.2 us -> 13.6 us
  starting transfers between devices: 2.57 us -> 6.78 us
    all_gather x2 -> x0, blocking collectives: 28.5 us -> none  [body(): rows = lax.all_gather(last_row[None], ('patch', 'sub'), axis=0, tiled=True)]
    ppermute x0 -> x6, waiting for transfers between devices: none -> 9.38 us  [grow_blocks(): lax.ppermute(blocks, axis, [(i, i ^ stride) for i in range(length)])]
    ppermute x0 -> x6, starting transfers between devices: none -> 4.21 us  [grow_blocks(): lax.ppermute(blocks, axis, [(i, i ^ stride) for i in range(length)])]
  transfers between devices with their start and end apart: 2 -> 8, of which waited for: 1 -> 5; matrix products, arithmetic and copies ran while one was open for 1% -> 2% of each run, Pallas kernels for 0% -> 0%
where the time goes in v1:
time: 138 us
  blocking collectives  88.9 us (64%)
  local copies, waits for them, and re-layouts  15.1 us (11%)
  waiting for transfers between devices  13.6 us (10%)
  other arithmetic  6.91 us (5%)
  starting transfers between devices  6.78 us (5%)
  between operations  6.21 us (4%)
    all_gather x2, blocking collectives, body(): lax.all_gather(first_row[None], ('patch', 'sub'), axis=0, tiled=True)  29.7 us
    all_gather x2, blocking collectives, body(): lax.all_gather(first_col[None], ('patch', 'sub'), axis=0, tiled=True)  29.7 us
    all_gather x2, blocking collectives, body(): cols = lax.all_gather(last_col[None], ('patch', 'sub'), axis=0, tiled=True)  29.6 us
    ppermute x6, waiting for transfers between devices, grow_blocks(): lax.ppermute(blocks, axis, [(i, i ^ stride) for i in range(length)])  9.38 us
    gather x2, local copies, waits for them, and re-layouts, body(): inflow = own_gain * jnp.take(received, own_table)  9.05 us
    ppermute x6, starting transfers between devices, grow_blocks(): lax.ppermute(blocks, axis, [(i, i ^ stride) for i in range(length)])  4.21 us
    ppermute x2, waiting for transfers between devices, passed_along(): lax.ppermute(value, axis, [(source, source + steps) for source in range(i...  4.2 us
    mul x2, other arithmetic, body(): mom_col = wet * (mom_col - courant * (south_eta - eta))  3.13 us
  transfers between devices with their start and end apart: 8, of which 5 were waited for; matrix products, arithmetic and copies ran while one was open for 2% of the time, Pallas kernels for 0%

profile of v1, /device:TPU:0, one launch (start us, length us, event | category | flops | bytes accessed | tf_op | source)
XLA Modules:
  0.0 137.5 jit_solution(8471939332566619102)
XLA Ops:
  0.6 0.0 copy-start
  0.6 1.0 copy.27
  1.7 1.3 collective-permute-start
  3.0 0.7 constant_dynamic-slice_fusion.4
  3.7 0.7 fusion.35
  4.4 0.7 copy-done.4
  7.7 4.5 %gather_fusion = f32[1024]{0:T(1024)S(1)} fusion(f32[1024]{0:T(1024)S(1)} %collective-permute-done, s32[1024]{0:T(1024)S(1)} %fusion.22), kind=kCustom, calls=%fused_computation.clone | custom fusion | bytes 12288 | tf_op jit(solution)/shard_map/jit(_take)/gather | solution.py:68
  12.2 15.7 %all-gather.2 = f32[8192]{0:T(1024)S(1)} all-gather(f32[1024]{0:T(1024)S(1)} %get-tuple-element.51), channel_id=4, replica_groups=mesh['parts'=2,'patch'=4,'level'=2,'sub'=2] {'patch','sub'}, dimensions={0}, use_global_device_ids=true | all-gather | bytes 36864 | tf_op jit(solution)/shard_map/all_gather | solution.py:74
  27.9 0.1 scatter-add.6
  28.0 0.2 slice.143
  28.3 0.0 copy-start.1
  28.3 14.8 %all-gather = f32[1024,1]{1,0:T(8,128)S(1)} all-gather(f32[128,1]{1,0:T(8,128)S(1)} %slice.144), channel_id=2, replica_groups=mesh['parts'=2,'patch'=4,'level'=2,'sub'=2] {'patch','sub'}, dimensions={0}, use_global_device_ids=true | all-gather | bytes 4608 | tf_op jit(solution)/shard_map/all_gather | solution.py:73
  43.1 0.2 reduce.4
  43.3 0.1 copy.17
  43.5 1.6 %fusion.9 = (f32[128,1024]{1,0:T(8,128)S(1)}, f32[128,1024]{1,0:T(8,128)S(1)}) fusion(f32[128,1024]{1,0:T(8,128)S(1)} %scatter-add.6, f32[1,1024]{1,0:T(1,128)S(1)} %bitcast.123, f32[127,1024]{1,0:T(8,128)S(1)} %slice.147, f32[2,1,128,1024]{3,2,1,0:T(8,128)} %param.18, s32[1,128,1024]{2,1,0:T(8,128)S(1)} %copy-done.1, f32[128,1]{1,0:T(8,128)S(1)} %copy.17, ...), kind=kLoop, calls=%fused_computation.15 | loop fusion | flops 1441792 | bytes 4194304 | tf_op jit(solution)/shard_map/mul | solution.py:85
  45.1 0.4 collective-permute-start.1
  45.5 0.8 collective-permute-done.1
  46.4 1.9 %collective-permute-start.2 = (f32[2,1,1024]{2,0,1:T(2,128)S(1)}, f32[2,1,1024]{2,0,1:T(2,128)S(1)}, u32[]{:S(2)}, u32[]{:S(2)}) collective-permute-start(f32[2,1,1024]{2,0,1:T(2,128)S(1)} %pad_maximum_fusion.2), channel_id=1, source_target_pairs={{0,4},{1,5},{4,0},{5,1},{8,12},{9,13},{12,8},{13,9},{2,6},{3,7},{6... | collective-permute-start | bytes 24584 | tf_op jit(solution)/shard_map/ppermute | solution.py:20
  50.8 0.1 slice.145
  50.9 14.8 %all-gather.1 = f32[1024,1]{1,0:T(8,128)S(1)} all-gather(f32[128,1]{1,0:T(8,128)S(1)} %slice.145), channel_id=3, replica_groups=mesh['parts'=2,'patch'=4,'level'=2,'sub'=2] {'patch','sub'}, dimensions={0}, use_global_device_ids=true | all-gather | bytes 4608 | tf_op jit(solution)/shard_map/all_gather | solution.py:88
  65.7 0.2 reduce.5
  65.9 0.0 collective-permute-done.2
  66.0 0.7 collective-permute-start.3
  66.7 0.1 copy.18
  66.8 3.9 %collective-permute-done.3 = f32[4,1,1024]{2,0,1:T(4,128)S(1)} collective-permute-done((f32[4,1,1024]{2,0,1:T(4,128)S(1)}, f32[4,1,1024]{2,0,1:T(4,128)S(1)}, u32[]{:S(2)}, u32[]{:S(2)}) %collective-permute-start.3) | collective-permute-done | bytes 16416 | tf_op jit(solution)/shard_map/ppermute | solution.py:20
  70.7 0.4 fusion.6
  71.2 1.3 collective-permute-start.4
  72.5 4.2 %collective-permute-done.4 = f32[1024]{0:T(1024)S(1)} collective-permute-done((f32[1024]{0:T(1024)S(1)}, f32[1024]{0:T(1024)S(1)}, u32[]{:S(2)}, u32[]{:S(2)}) %collective-permute-start.4) | collective-permute-done | bytes 4128 | tf_op jit(solution)/shard_map/ppermute | solution.py:32
  76.7 4.5 %gather_fusion.1 = f32[1024]{0:T(1024)S(1)} fusion(f32[1024]{0:T(1024)S(1)} %collective-permute-done.4, s32[1024]{0:T(1024)S(1)} %fusion.22), kind=kCustom, calls=%fused_computation.1.clone | custom fusion | bytes 12288 | tf_op jit(solution)/shard_map/jit(_take)/gather | solution.py:68
  81.2 0.1 scatter-add.9
  81.4 0.8 slice.155
  82.2 1.0 slice.151
  83.2 14.0 %all-gather.5 = f32[8,1,1024]{2,1,0:T(1,128)S(1)} all-gather(f32[1,1,1024]{2,1,0:T(1,128)S(1)} %bitcast.115), channel_id=1, replica_groups=mesh['parts'=2,'patch'=4,'level'=2,'sub'=2] {'patch','sub'}, dimensions={0}, use_global_device_ids=true | all-gather | bytes 36864 | tf_op jit(solution)/shard_map/all_gather | solution.py:74
  97.2 14.8 %all-gather.3 = f32[1024,1]{1,0:T(8,128)S(1)} all-gather(f32[128,1]{1,0:T(8,128)S(1)} %slice.152), channel_id=5, replica_groups=mesh['parts'=2,'patch'=4,'level'=2,'sub'=2] {'patch','sub'}, dimensions={0}, use_global_device_ids=true | all-gather | bytes 4608 | tf_op jit(solution)/shard_map/all_gather | solution.py:73
  112.0 0.2 reduce.6
  112.3 0.1 copy.19
  112.4 1.6 %fusion.20 = (f32[128,1024]{1,0:T(8,128)S(1)}, f32[128,1024]{1,0:T(8,128)S(1)}) fusion(f32[128,1024]{1,0:T(8,128)S(1)} %get-tuple-element.53, f32[128,1024]{1,0:T(8,128)S(1)} %scatter-add.9, f32[1,1024]{1,0:T(1,128)S(1)} %bitcast.121, f32[127,1024]{1,0:T(8,128)} %slice.155, s32[1,128,1024]{2,1,0:T(8,128)S(1)} %copy-done.1, ...), kind=kLoop, calls=%fused_computation.30 | loop fusion | flops 1441792 | bytes 4194304 | tf_op jit(solution)/shard_map/mul | solution.py:85
  114.0 0.4 collective-permute-start.5
  114.4 0.8 collective-permute-done.5
  115.2 0.1 collective-permute-start.6
  115.3 1.0 maximum_bitcast_fusion
  116.3 0.1 slice.153
  116.4 14.8 %all-gather.4 = f32[1024,1]{1,0:T(8,128)S(1)} all-gather(f32[128,1]{1,0:T(8,128)S(1)} %slice.153), channel_id=6, replica_groups=mesh['parts'=2,'patch'=4,'level'=2,'sub'=2] {'patch','sub'}, dimensions={0}, use_global_device_ids=true | all-gather | bytes 4608 | tf_op jit(solution)/shard_map/all_gather | solution.py:88
  131.2 0.2 reduce.7
  131.5 0.7 collective-permute-start.7
  132.2 0.1 copy.20
  132.3 3.9 %collective-permute-done.7 = f32[4,1,1024]{2,0,1:T(4,128)S(1)} collective-permute-done((f32[4,1,1024]{2,0,1:T(4,128)S(1)}, f32[4,1,1024]{2,0,1:T(4,128)S(1)}, u32[]{:S(2)}, u32[]{:S(2)}) %collective-permute-start.7) | collective-permute-done | bytes 16416 | tf_op jit(solution)/shard_map/ppermute | solution.py:20
  136.3 1.2 fusion.17
  (48 shorter events, 0.4 us)
Async XLA Ops:
  0.6 3.7 %copy-start = (s32[2,1024]{1,0:T(2,128)S(1)}, s32[2,1024]{1,0:T(2,128)}, u32[]{:S(2)}) copy-start(s32[2,1024]{1,0:T(2,128)} %param.23) | copy-start | bytes 24580
  1.7 6.0 %collective-permute-start = (f32[1024]{0:T(1024)S(1)}, f32[1024]{0:T(1024)S(1)}, u32[]{:S(2)}, u32[]{:S(2)}) collective-permute-start(f32[1024]{0:T(1024)S(1)} %bitcast.126), channel_id=1, source_target_pairs={{2,0},{3,1},{6,4},{7,5},{10,8},{11,9},{14,12},{15,13},{18,16},{19,... | collective-permute-start | bytes 12296 | tf_op jit(solution)/shard_map/ppermute | solution.py:32
  4.3 0.7 copy-start.4
  28.3 15.2 %copy-start.1 = (s32[1,128,1024]{2,1,0:T(8,128)S(1)}, s32[1,128,1024]{2,1,0:T(8,128)}, u32[]{:S(2)}) copy-start(s32[1,128,1024]{2,1,0:T(8,128)} %param.20) | copy-start | bytes 1572868
  45.1 1.2 collective-permute-start.1
  46.4 19.5 %collective-permute-start.2 = (f32[2,1,1024]{2,0,1:T(2,128)S(1)}, f32[2,1,1024]{2,0,1:T(2,128)S(1)}, u32[]{:S(2)}, u32[]{:S(2)}) collective-permute-start(f32[2,1,1024]{2,0,1:T(2,128)S(1)} %pad_maximum_fusion.2), channel_id=1, source_target_pairs={{0,4},{1,5},{4,0},{5,1},{8,12},{9,13},{12,8},{13,9},{2,6},{3,7},{6... | collective-permute-start | bytes 24584 | tf_op jit(solution)/shard_map/ppermute | solution.py:20
  65.7 5.0 %copy-start.2 = (f32[1,128,1024]{2,1,0:T(8,128)S(1)}, f32[1,128,1024]{2,1,0:T(8,128)}, u32[]{:S(2)}) copy-start(f32[1,128,1024]{2,1,0:T(8,128)} %param.19) | copy-start | bytes 1572868
  66.0 4.7 %collective-permute-start.3 = (f32[4,1,1024]{2,0,1:T(4,128)S(1)}, f32[4,1,1024]{2,0,1:T(4,128)S(1)}, u32[]{:S(2)}, u32[]{:S(2)}) collective-permute-start(f32[4,1,1024]{2,0,1:T(4,128)S(1)} %pad_maximum_fusion), channel_id=1, source_target_pairs={{0,8},{1,9},{4,12},{5,13},{8,0},{9,1},{12,4},{13,5},{2,10},{3,11},... | collective-permute-start | bytes 49160 | tf_op jit(solution)/shard_map/ppermute | solution.py:20
  71.2 5.5 %collective-permute-start.4 = (f32[1024]{0:T(1024)S(1)}, f32[1024]{0:T(1024)S(1)}, u32[]{:S(2)}, u32[]{:S(2)}) collective-permute-start(f32[1024]{0:T(1024)S(1)} %bitcast.140), channel_id=1, source_target_pairs={{2,0},{3,1},{6,4},{7,5},{10,8},{11,9},{14,12},{15,13},{18,16},{19,... | collective-permute-start | bytes 12296 | tf_op jit(solution)/shard_map/ppermute | solution.py:32
  114.0 1.2 collective-permute-start.5
  115.2 16.2 %collective-permute-start.6 = (f32[2,1,1024]{2,0,1:T(2,128)S(1)}, f32[2,1,1024]{2,0,1:T(2,128)S(1)}, u32[]{:S(2)}, u32[]{:S(2)}) collective-permute-start(f32[2,1,1024]{2,0,1:T(2,128)S(1)} %pad_maximum_fusion.3), channel_id=1, source_target_pairs={{0,4},{1,5},{4,0},{5,1},{8,12},{9,13},{12,8},{13,9},{2,6},{3,7},{6... | collective-permute-start | bytes 24584 | tf_op jit(solution)/shard_map/ppermute | solution.py:20
  131.2 5.0 %copy-start.3 = (f32[1,128,1024]{2,1,0:T(8,128)S(1)}, f32[1,128,1024]{2,1,0:T(8,128)}, u32[]{:S(2)}) copy-start(f32[1,128,1024]{2,1,0:T(8,128)} %param.19) | copy-start | bytes 1572868
  131.5 4.7 %collective-permute-start.7 = (f32[4,1,1024]{2,0,1:T(4,128)S(1)}, f32[4,1,1024]{2,0,1:T(4,128)S(1)}, u32[]{:S(2)}, u32[]{:S(2)}) collective-permute-start(f32[4,1,1024]{2,0,1:T(4,128)S(1)} %pad_maximum_fusion.1), channel_id=1, source_target_pairs={{0,8},{1,9},{4,12},{5,13},{8,0},{9,1},{12,4},{13,5},{2,10},{3,11},... | collective-permute-start | bytes 49160 | tf_op jit(solution)/shard_map/ppermute | solution.py:20
